TPU v7x, 128 devices: a whole 4x4x4 slice. The times are simulated.
128 devices in a mesh: node: 4 (over y_hi, core), hst: 32 (over y_lo, x, z).
Axes of the slice: x: 4, y: 4 (y_hi: 2, y_lo: 2; y = y_hi * 2 + y_lo), z: 4, core: 2. Of those that a mesh axis runs over, the one named last changes fastest.
Arguments:
- hidden: bfloat16 [32, 4096, 640], P('hst', 'node'), may hold values from -6 to 6
- cotangent: bfloat16 [32, 4096, 4608], P('hst', 'node'), may hold values from -12 to 12
- anchor: float32 [32, 640, 4608], P('hst', 'node'), may hold values from -0.25 to 0.25
- momentum: float32 [32, 640, 4608], P('hst', 'node'), may hold values from -0.6 to 0.6
- round_mask: int32 [1], replicated, may hold values from 1 to 31
Outputs:
- weights_out: bfloat16 [32, 640, 4608], P('hst')
- momentum_out: float32 [32, 640, 4608], P('hst', 'node')
Inputs may be any that keep to these rules, and one draw needn't show every extreme that they name: round_mask is the same for all hosts; host i averages with the hosts i XOR s for every s whose bits lie within round_mask.
All inputs are finite; a program needn't handle non-finite values.
Results may differ from a plain program's by a relative error of at most 0.009.
Values may be sent and summed in bfloat16 or wider, within the bound.
A program may use at most 256 MiB of HBM per device.

v0:
```python
import jax
import jax.numpy as jnp
from jax import lax
from jax.sharding import PartitionSpec as P

base_rate = 0.5
slow_rate = 1.0
slow_beta = 0.7


def swapped(block, axis, bit):
    count = lax.axis_size(axis)
    route = []
    for low in range(count):
        high = low | 1 << bit
        if high != low and high < count:
            route += [(low, high), (high, low)]
    return lax.ppermute(block, axis, route)


def half_step(current, bit_index):
    other_rows = swapped(current.astype(jnp.bfloat16), "hst", bit_index).astype(current.dtype)
    return 0.5 * (current + other_rows)


def local(hidden, cotangent, anchor, momentum, round_mask):
    tokens_here = hidden[0]
    grads_in = cotangent[0]
    token_scale = 1.0 / (tokens_here.shape[0] * lax.axis_size("node"))
    product = lax.dot_general(
        tokens_here, grads_in, (((0,), (0,)), ((), ())), preferred_element_type=jnp.float32
    )
    gradient = lax.psum_scatter(
        (product * token_scale).astype(jnp.bfloat16), "node", scatter_dimension=0, tiled=True
    ).astype(jnp.float32)
    stepped = anchor[0] - base_rate * gradient
    mask_value = round_mask[0]
    host_count = lax.axis_size("hst")
    bit_count = host_count.bit_length() - 1
    bit_list = list(range(bit_count))
    averaged = stepped
    for bit_index in bit_list:
        active = jnp.bitwise_and(jnp.right_shift(mask_value, bit_index), 1) == 1
        averaged = jnp.where(active, half_step(averaged, bit_index), averaged)
    momentum_new = slow_beta * momentum[0] + (anchor[0] - averaged) / base_rate
    updated = (anchor[0] - slow_rate * base_rate * momentum_new).astype(jnp.bfloat16)
    weights_whole = lax.all_gather(updated[None], "node", axis=1, tiled=True)
    return (weights_whole, momentum_new[None])


def solution(mesh):
    placed = (
        P("hst", "node", None),
        P("hst", "node", None),
        P("hst", "node", None),
        P("hst", "node", None),
        P(),
    )
    return jax.shard_map(
        local,
        mesh=mesh,
        in_specs=placed,
        out_specs=(P("hst", None, None), P("hst", "node", None)),
        check_vma=False,
    )
```

profile of v0, /device:TPU:1, one launch (start us, length us, event | category | flops | bytes accessed | tf_op | source)
XLA Modules:
  0.0 318.9 jit_solution(657283550039399668)
XLA Ops:
  7.2 0.0 copy-start
  7.2 0.0 reduce-scatter.2.cloned.1.call-start
  7.2 1.3 copy-done
  8.5 10.5 %multiply_convert_fusion = bf16[640,4608]{1,0:T(8,128)(2,1)} fusion(bf16[1,1024,4608]{2,1,0:T(8,128)(2,1)} %param.6, bf16[1,1024,640]{2,1,0:T(8,128)(2,1)S(1)} %copy-done), kind=kOutput, calls=%fused_computation | convolution fusion | flops 6045696000 | bytes 16646144 | tf_op jit(solution)/shard_map/dot_general | solution.py:30
  19.0 0.0 reduce-scatter.2.cloned.1.call-update
  19.0 0.0 all-gather.3.cloned.1.call-start
  19.0 66.0 %reduce-scatter.2.cloned.1.call-done = bf16[160,4608]{1,0:T(8,128)(2,1)} async-done(((bf16[640,4608]{1,0:T(8,128)(2,1)}), bf16[160,4608]{1,0:T(8,128)(2,1)}) %reduce-scatter.2.cloned.1.call-update) | async-done | bytes 1474576 | tf_op jit(solution)/shard_map/reduce_scatter | solution.py:33
  85.0 0.0 copy-start.1
  85.0 0.0 copy-start.2
  85.0 2.8 fusion.6
  87.8 1.3 collective-permute-start
  89.8 31.2 %collective-permute-done = bf16[160,4608]{1,0:T(8,128)(2,1)S(1)} collective-permute-done((bf16[160,4608]{1,0:T(8,128)(2,1)S(1)}, bf16[160,4608]{1,0:T(8,128)(2,1)S(1)}, u32[]{:S(2)}, u32[]{:S(2)}) %collective-permute-start) | collective-permute-done | bytes 1474592 | tf_op jit(solution)/shard_map/ppermute | solution.py:18
  121.1 0.0 copy-done.1
  121.1 0.0 copy-done.2
  121.1 0.7 fusion.11
  121.8 2.9 collective-permute-start.1
  124.7 30.9 %collective-permute-done.1 = bf16[160,4608]{1,0:T(8,128)(2,1)S(1)} collective-permute-done((bf16[160,4608]{1,0:T(8,128)(2,1)S(1)}, bf16[160,4608]{1,0:T(8,128)(2,1)S(1)}, u32[]{:S(2)}, u32[]{:S(2)}) %collective-permute-start.1) | collective-permute-done | bytes 1474592 | tf_op jit(solution)/shard_map/ppermute | solution.py:18
  155.6 0.4 fusion.7
  156.0 1.2 collective-permute-start.2
  157.3 30.2 %collective-permute-done.2 = bf16[160,4608]{1,0:T(8,128)(2,1)S(1)} collective-permute-done((bf16[160,4608]{1,0:T(8,128)(2,1)S(1)}, bf16[160,4608]{1,0:T(8,128)(2,1)S(1)}, u32[]{:S(2)}, u32[]{:S(2)}) %collective-permute-start.2) | collective-permute-done | bytes 1474592 | tf_op jit(solution)/shard_map/ppermute | solution.py:18
  187.4 0.8 fusion.10
  188.3 2.7 collective-permute-start.3
  191.0 29.2 %collective-permute-done.3 = bf16[160,4608]{1,0:T(8,128)(2,1)S(1)} collective-permute-done((bf16[160,4608]{1,0:T(8,128)(2,1)S(1)}, bf16[160,4608]{1,0:T(8,128)(2,1)S(1)}, u32[]{:S(2)}, u32[]{:S(2)}) %collective-permute-start.3) | collective-permute-done | bytes 1474592 | tf_op jit(solution)/shard_map/ppermute | solution.py:18
  220.2 0.0 copy-start.3
  220.2 0.4 fusion.8
  220.7 0.3 collective-permute-start.4
  221.0 29.2 %collective-permute-done.4 = bf16[160,4608]{1,0:T(8,128)(2,1)S(1)} collective-permute-done((bf16[160,4608]{1,0:T(8,128)(2,1)S(1)}, bf16[160,4608]{1,0:T(8,128)(2,1)S(1)}, u32[]{:S(2)}, u32[]{:S(2)}) %collective-permute-start.4) | collective-permute-done | bytes 1474592 | tf_op jit(solution)/shard_map/ppermute | solution.py:18
  250.2 0.0 copy-done.3
  250.2 3.5 %fusion.5 = (bf16[160,4608]{1,0:T(8,128)(2,1)}, f32[160,4608]{1,0:T(8,128)}) fusion(f32[1,160,4608]{2,1,0:T(8,128)S(1)} %copy-done.1, bf16[160,4608]{1,0:T(8,128)(2,1)S(1)} %collective-permute-done.4, f32[160,4608]{1,0:T(8,128)S(1)} %get-tuple-element.5, bf16[160,4608]{1,0:T(8,128)(2,1)S(1)} %collective-permute-done.3, pred[]{:T(512)} %bitcast.3, ...), kind=kLoop, calls=%fused_computation.8 | loop fusion | flops 11059200 | bytes 16220162 | tf_op jit(solution)/shard_map/convert_element_type | solution.py:46
  253.7 0.0 all-gather.3.cloned.1.call-update
  253.7 52.7 %all-gather.3.cloned.1.call-done = bf16[640,4608]{1,0:T(8,128)(2,1)} async-done(((bf16[160,4608]{1,0:T(8,128)(2,1)}), bf16[640,4608]{1,0:T(8,128)(2,1)}) %all-gather.3.cloned.1.call-update) | async-done | bytes 5898256 | tf_op jit(solution)/shard_map/all_gather | solution.py:47
  306.4 5.6 %copy.9 = bf16[1,640,4608]{2,1,0:T(8,128)(2,1)} copy(bf16[1,640,4608]{2,1,0:T(8,128)(2,1)} %bitcast.34) | data formatting | bytes 11796480
Async XLA Ops:
  7.2 1.3 copy-start
  7.2 77.9 %reduce-scatter.2.cloned.1.call-start = ((), (), s32[]{:S(2)}) async-start(), calls=%async_computation.1 | async-start | bytes 7372800 | tf_op jit(solution)/shard_map/reduce_scatter | solution.py:33
  19.0 287.4 %all-gather.3.cloned.1.call-start = ((), (), s32[]{:S(2)}) async-start(), calls=%async_computation.2 | async-start | bytes 7372800 | tf_op jit(solution)/shard_map/all_gather | solution.py:47
  85.0 36.0 %copy-start.1 = (f32[1,160,4608]{2,1,0:T(8,128)S(1)}, f32[1,160,4608]{2,1,0:T(8,128)}, u32[]{:S(2)}) copy-start(f32[1,160,4608]{2,1,0:T(8,128)} %param.7) | copy-start | bytes 8847364
  85.0 36.0 %copy-start.2 = (bf16[160,4608]{1,0:T(8,128)(2,1)S(1)}, bf16[160,4608]{1,0:T(8,128)(2,1)}, u32[]{:S(2)}) copy-start(bf16[160,4608]{1,0:T(8,128)(2,1)} %reduce-scatter.2.cloned.1.call-done) | copy-start | bytes 4423684
  87.8 33.2 %collective-permute-start = (bf16[160,4608]{1,0:T(8,128)(2,1)S(1)}, bf16[160,4608]{1,0:T(8,128)(2,1)S(1)}, u32[]{:S(2)}, u32[]{:S(2)}) collective-permute-start(bf16[160,4608]{1,0:T(8,128)(2,1)S(1)} %fusion.6), channel_id=1, source_target_pairs={{0,1},{1,0},{2,3},{3,2},{4,5},{5,4},{6,7},{7,6},{8,9},{9,8},{10,11... | collective-permute-start | bytes 4423688 | tf_op jit(solution)/shard_map/ppermute | solution.py:18
  121.8 33.8 %collective-permute-start.1 = (bf16[160,4608]{1,0:T(8,128)(2,1)S(1)}, bf16[160,4608]{1,0:T(8,128)(2,1)S(1)}, u32[]{:S(2)}, u32[]{:S(2)}) collective-permute-start(bf16[160,4608]{1,0:T(8,128)(2,1)S(1)} %get-tuple-element.6), channel_id=1, source_target_pairs={{0,2},{2,0},{1,3},{3,1},{4,6},{6,4},{5,7},{7,5},{8,10},{10,8},{9,1... | collective-permute-start | bytes 4423688 | tf_op jit(solution)/shard_map/ppermute | solution.py:18
  156.0 31.4 %collective-permute-start.2 = (bf16[160,4608]{1,0:T(8,128)(2,1)S(1)}, bf16[160,4608]{1,0:T(8,128)(2,1)S(1)}, u32[]{:S(2)}, u32[]{:S(2)}) collective-permute-start(bf16[160,4608]{1,0:T(8,128)(2,1)S(1)} %fusion.7), channel_id=1, source_target_pairs={{0,4},{4,0},{1,5},{5,1},{2,6},{6,2},{3,7},{7,3},{8,12},{12,8},{9,1... | collective-permute-start | bytes 4423688 | tf_op jit(solution)/shard_map/ppermute | solution.py:18
  188.3 32.0 %collective-permute-start.3 = (bf16[160,4608]{1,0:T(8,128)(2,1)S(1)}, bf16[160,4608]{1,0:T(8,128)(2,1)S(1)}, u32[]{:S(2)}, u32[]{:S(2)}) collective-permute-start(bf16[160,4608]{1,0:T(8,128)(2,1)S(1)} %get-tuple-element.4), channel_id=1, source_target_pairs={{0,8},{8,0},{1,9},{9,1},{2,10},{10,2},{3,11},{11,3},{4,12},{12,4},... | collective-permute-start | bytes 4423688 | tf_op jit(solution)/shard_map/ppermute | solution.py:18
  220.2 30.0 %copy-start.3 = (f32[1,160,4608]{2,1,0:T(8,128)S(1)}, f32[1,160,4608]{2,1,0:T(8,128)}, u32[]{:S(2)}) copy-start(f32[1,160,4608]{2,1,0:T(8,128)} %param.8) | copy-start | bytes 8847364
  220.7 29.6 %collective-permute-start.4 = (bf16[160,4608]{1,0:T(8,128)(2,1)S(1)}, bf16[160,4608]{1,0:T(8,128)(2,1)S(1)}, u32[]{:S(2)}, u32[]{:S(2)}) collective-permute-start(bf16[160,4608]{1,0:T(8,128)(2,1)S(1)} %fusion.8), channel_id=1, source_target_pairs={{0,16},{16,0},{1,17},{17,1},{2,18},{18,2},{3,19},{19,3},{4,20},{20... | collective-permute-start | bytes 4423688 | tf_op jit(solution)/shard_map/ppermute | solution.py:18
Sparse Core Ops, SparseCore 0:
  19.1 65.8 reduce-scatter.1
  253.8 52.5 all-gather.2
where the time goes:
time: 319 us
  waiting for transfers between devices  269 us (84%)
  between operations  14.7 us (5%)
  matrix products  10.5 us (3%)
  starting transfers between devices  8.68 us (3%)
  other arithmetic  8.62 us (3%)
  local copies, waits for them, and re-layouts  6.9 us (2%)
    ppermute x5, waiting for transfers between devices, swapped(): return lax.ppermute(block, axis, route)  151 us
    reduce_scatter x1, waiting for transfers between devices, local(): lax.psum_scatter((product * token_scale).astype(jnp.bfloat16), 'node', sc...  66 us
    all_gather x1, waiting for transfers between devices, local(): weights_whole = lax.all_gather(updated[None], 'node', axis=1, tiled=True)  52.7 us
    dot_general x1, matrix products, local(): lax.dot_general(tokens_here, grads_in, (((0,), (0,)), ((), ())), preferre...  10.5 us
    ppermute x5, starting transfers between devices, swapped(): return lax.ppermute(block, axis, route)  8.6 us
    unnamed x9, local copies, waits for them, and re-layouts  6.9 us
  transfers between devices with their start and end apart: 7, of which 7 were waited for; matrix products, arithmetic and copies ran while one was open for 0% of the time, Pallas kernels for 0%

commit v1 on v0

--- a/solution.py
+++ b/solution.py
@@ -44,7 +44,9 @@
         averaged = jnp.where(active, half_step(averaged, bit_index), averaged)
     momentum_new = slow_beta * momentum[0] + (anchor[0] - averaged) / base_rate
     updated = (anchor[0] - slow_rate * base_rate * momentum_new).astype(jnp.bfloat16)
-    weights_whole = lax.all_gather(updated[None], "node", axis=1, tiled=True)
+    block_2 = updated[None]
+    outgoing = jnp.stack([block_2] * lax.axis_size("node"))
+    weights_whole = jnp.concatenate(lax.all_to_all(outgoing, "node", 0, 0), axis=1)
     return (weights_whole, momentum_new[None])
 
 

time: 319 us -> 338 us (1.060)
  blocking collectives: 0 us -> 74.8 us
  waiting for transfers between devices: 269 us -> 217 us
    all_to_all x0 -> x1, blocking collectives: none -> 74.8 us  [local(): lax.all_to_all(outgoing, 'node', 0, 0)]
    all_gather x1 -> x0, waiting for transfers between devices: 52.7 us -> none  [local(): weights_whole = lax.all_gather(updated[None], 'node', axis=1, tiled=True)]
  transfers between devices with their start and end apart: 7 -> 6, of which waited for: 7 -> 6; matrix products, arithmetic and copies ran while one was open for 0% -> 0% of each run, Pallas kernels for 0% -> 0%
where the time goes in v1:
time: 338 us
  waiting for transfers between devices  217 us (64%)
  blocking collectives  74.8 us (22%)
  between operations  14.7 us (4%)
  matrix products  10.5 us (3%)
  starting transfers between devices  8.64 us (3%)
  other arithmetic  8.14 us (2%)
  local copies, waits for them, and re-layouts  4.32 us (1%)
    ppermute x5, waiting for transfers between devices, swapped(): return lax.ppermute(block, axis, route)  151 us
    all_to_all x1, blocking collectives, local(): lax.all_to_all(outgoing, 'node', 0, 0)  74.8 us
    reduce_scatter x1, waiting for transfers between devices, local(): lax.psum_scatter((product * token_scale).astype(jnp.bfloat16), 'node', sc...  66 us
    dot_general x1, matrix products, local(): lax.dot_general(tokens_here, grads_in, (((0,), (0,)), ((), ())), preferre...  10.5 us
    ppermute x5, starting transfers between devices, swapped(): return lax.ppermute(block, axis, route)  8.6 us
  transfers between devices with their start and end apart: 6, of which 6 were waited for; matrix products, arithmetic and copies ran while one was open for 0% of the time, Pallas kernels for 0%

profile of v1, /device:TPU:1, one launch (start us, length us, event | category | flops | bytes accessed | tf_op | source)
XLA Modules:
  0.0 337.9 jit_solution(8404988346136414491)
XLA Ops:
  7.2 0.0 copy-start
  7.2 0.0 reduce-scatter.2.cloned.1.call-start
  7.2 1.3 copy-done
  8.5 10.5 %multiply_convert_fusion = bf16[640,4608]{1,0:T(8,128)(2,1)} fusion(bf16[1,1024,4608]{2,1,0:T(8,128)(2,1)} %param.6, bf16[1,1024,640]{2,1,0:T(8,128)(2,1)S(1)} %copy-done), kind=kOutput, calls=%fused_computation | convolution fusion | flops 6045696000 | bytes 16646144 | tf_op jit(solution)/shard_map/dot_general | solution.py:30
  19.0 0.0 reduce-scatter.2.cloned.1.call-update
  19.0 66.0 %reduce-scatter.2.cloned.1.call-done = bf16[160,4608]{1,0:T(8,128)(2,1)} async-done(((bf16[640,4608]{1,0:T(8,128)(2,1)}), bf16[160,4608]{1,0:T(8,128)(2,1)}) %reduce-scatter.2.cloned.1.call-update) | async-done | bytes 1474576 | tf_op jit(solution)/shard_map/reduce_scatter | solution.py:33
  85.0 0.0 copy-start.1
  85.0 0.0 copy-start.2
  85.0 2.8 fusion.6
  87.8 1.3 collective-permute-start
  89.8 31.2 %collective-permute-done = bf16[160,4608]{1,0:T(8,128)(2,1)S(1)} collective-permute-done((bf16[160,4608]{1,0:T(8,128)(2,1)S(1)}, bf16[160,4608]{1,0:T(8,128)(2,1)S(1)}, u32[]{:S(2)}, u32[]{:S(2)}) %collective-permute-start) | collective-permute-done | bytes 1474592 | tf_op jit(solution)/shard_map/ppermute | solution.py:18
  121.1 0.0 copy-done.1
  121.1 0.0 copy-done.2
  121.1 0.7 fusion.11
  121.8 2.9 collective-permute-start.1
  124.7 30.9 %collective-permute-done.1 = bf16[160,4608]{1,0:T(8,128)(2,1)S(1)} collective-permute-done((bf16[160,4608]{1,0:T(8,128)(2,1)S(1)}, bf16[160,4608]{1,0:T(8,128)(2,1)S(1)}, u32[]{:S(2)}, u32[]{:S(2)}) %collective-permute-start.1) | collective-permute-done | bytes 1474592 | tf_op jit(solution)/shard_map/ppermute | solution.py:18
  155.6 0.4 fusion.7
  156.0 1.2 collective-permute-start.2
  157.3 30.2 %collective-permute-done.2 = bf16[160,4608]{1,0:T(8,128)(2,1)S(1)} collective-permute-done((bf16[160,4608]{1,0:T(8,128)(2,1)S(1)}, bf16[160,4608]{1,0:T(8,128)(2,1)S(1)}, u32[]{:S(2)}, u32[]{:S(2)}) %collective-permute-start.2) | collective-permute-done | bytes 1474592 | tf_op jit(solution)/shard_map/ppermute | solution.py:18
  187.4 0.8 fusion.10
  188.3 2.7 collective-permute-start.3
  191.0 29.2 %collective-permute-done.3 = bf16[160,4608]{1,0:T(8,128)(2,1)S(1)} collective-permute-done((bf16[160,4608]{1,0:T(8,128)(2,1)S(1)}, bf16[160,4608]{1,0:T(8,128)(2,1)S(1)}, u32[]{:S(2)}, u32[]{:S(2)}) %collective-permute-start.3) | collective-permute-done | bytes 1474592 | tf_op jit(solution)/shard_map/ppermute | solution.py:18
  220.2 0.0 copy-start.3
  220.2 0.4 fusion.8
  220.7 0.3 collective-permute-start.4
  221.0 29.2 %collective-permute-done.4 = bf16[160,4608]{1,0:T(8,128)(2,1)S(1)} collective-permute-done((bf16[160,4608]{1,0:T(8,128)(2,1)S(1)}, bf16[160,4608]{1,0:T(8,128)(2,1)S(1)}, u32[]{:S(2)}, u32[]{:S(2)}) %collective-permute-start.4) | collective-permute-done | bytes 1474592 | tf_op jit(solution)/shard_map/ppermute | solution.py:18
  250.2 0.0 copy-done.3
  250.2 3.0 fusion.5
  253.2 0.5 stack.3
  253.7 74.8 %all_to_all.5 = bf16[4,1,160,4608]{3,2,1,0:T(8,128)(2,1)S(1)} all-to-all(bf16[4,1,160,4608]{3,2,1,0:T(8,128)(2,1)S(1)} %stack.3), channel_id=1, replica_groups=mesh['node'=4,'hst'=32] {'node'}, dimensions={0} | all-to-all | bytes 11796480 | tf_op jit(solution)/shard_map/all_to_all | solution.py:49
  328.4 2.6 copy.9
Async XLA Ops:
  7.2 1.3 copy-start
  7.2 77.9 %reduce-scatter.2.cloned.1.call-start = ((), (), s32[]{:S(2)}) async-start(), calls=%async_computation.2 | async-start | bytes 7372800 | tf_op jit(solution)/shard_map/reduce_scatter | solution.py:33
  85.0 36.0 %copy-start.1 = (f32[1,160,4608]{2,1,0:T(8,128)S(1)}, f32[1,160,4608]{2,1,0:T(8,128)}, u32[]{:S(2)}) copy-start(f32[1,160,4608]{2,1,0:T(8,128)} %param.7) | copy-start | bytes 8847364
  85.0 36.0 %copy-start.2 = (bf16[160,4608]{1,0:T(8,128)(2,1)S(1)}, bf16[160,4608]{1,0:T(8,128)(2,1)}, u32[]{:S(2)}) copy-start(bf16[160,4608]{1,0:T(8,128)(2,1)} %reduce-scatter.2.cloned.1.call-done) | copy-start | bytes 4423684
  87.8 33.2 %collective-permute-start = (bf16[160,4608]{1,0:T(8,128)(2,1)S(1)}, bf16[160,4608]{1,0:T(8,128)(2,1)S(1)}, u32[]{:S(2)}, u32[]{:S(2)}) collective-permute-start(bf16[160,4608]{1,0:T(8,128)(2,1)S(1)} %fusion.6), channel_id=1, source_target_pairs={{0,1},{1,0},{2,3},{3,2},{4,5},{5,4},{6,7},{7,6},{8,9},{9,8},{10,11... | collective-permute-start | bytes 4423688 | tf_op jit(solution)/shard_map/ppermute | solution.py:18
  121.8 33.8 %collective-permute-start.1 = (bf16[160,4608]{1,0:T(8,128)(2,1)S(1)}, bf16[160,4608]{1,0:T(8,128)(2,1)S(1)}, u32[]{:S(2)}, u32[]{:S(2)}) collective-permute-start(bf16[160,4608]{1,0:T(8,128)(2,1)S(1)} %get-tuple-element.6), channel_id=1, source_target_pairs={{0,2},{2,0},{1,3},{3,1},{4,6},{6,4},{5,7},{7,5},{8,10},{10,8},{9,1... | collective-permute-start | bytes 4423688 | tf_op jit(solution)/shard_map/ppermute | solution.py:18
  156.0 31.4 %collective-permute-start.2 = (bf16[160,4608]{1,0:T(8,128)(2,1)S(1)}, bf16[160,4608]{1,0:T(8,128)(2,1)S(1)}, u32[]{:S(2)}, u32[]{:S(2)}) collective-permute-start(bf16[160,4608]{1,0:T(8,128)(2,1)S(1)} %fusion.7), channel_id=1, source_target_pairs={{0,4},{4,0},{1,5},{5,1},{2,6},{6,2},{3,7},{7,3},{8,12},{12,8},{9,1... | collective-permute-start | bytes 4423688 | tf_op jit(solution)/shard_map/ppermute | solution.py:18
  188.3 32.0 %collective-permute-start.3 = (bf16[160,4608]{1,0:T(8,128)(2,1)S(1)}, bf16[160,4608]{1,0:T(8,128)(2,1)S(1)}, u32[]{:S(2)}, u32[]{:S(2)}) collective-permute-start(bf16[160,4608]{1,0:T(8,128)(2,1)S(1)} %get-tuple-element.4), channel_id=1, source_target_pairs={{0,8},{8,0},{1,9},{9,1},{2,10},{10,2},{3,11},{11,3},{4,12},{12,4},... | collective-permute-start | bytes 4423688 | tf_op jit(solution)/shard_map/ppermute | solution.py:18
  220.2 30.0 %copy-start.3 = (f32[1,160,4608]{2,1,0:T(8,128)S(1)}, f32[1,160,4608]{2,1,0:T(8,128)}, u32[]{:S(2)}) copy-start(f32[1,160,4608]{2,1,0:T(8,128)} %param.8) | copy-start | bytes 8847364
  220.7 29.6 %collective-permute-start.4 = (bf16[160,4608]{1,0:T(8,128)(2,1)S(1)}, bf16[160,4608]{1,0:T(8,128)(2,1)S(1)}, u32[]{:S(2)}, u32[]{:S(2)}) collective-permute-start(bf16[160,4608]{1,0:T(8,128)(2,1)S(1)} %fusion.8), channel_id=1, source_target_pairs={{0,16},{16,0},{1,17},{17,1},{2,18},{18,2},{3,19},{19,3},{4,20},{20... | collective-permute-start | bytes 4423688 | tf_op jit(solution)/shard_map/ppermute | solution.py:18
Sparse Core Ops, SparseCore 0:
  19.1 65.8 reduce-scatter.1
